TPU v7x, 32 devices: a whole 2x2x4 slice. The times are simulated.
32 devices in a mesh: grp: 8 (over z, y), row: 4 (over x, core).
Axes of the slice: x: 2, y: 2, z: 4, core: 2. Of those that a mesh axis runs over, the one named last changes fastest.
Arguments:
- view_a: float32 [4096, 8192], P('row', 'grp'), may hold values from -40 to 40
- view_b: float32 [4096, 8192], P('row', 'grp'), may hold values from -40 to 40
Outputs:
- grad_a: float32 [4096, 8192], P('row', 'grp')
- grad_b: float32 [4096, 8192], P('row', 'grp')
All inputs are finite; a program needn't handle non-finite values.
Results may differ from a plain program's by a relative error of at most 0.00025.
Values sent between devices are 32-bit elements; how exact they have to be, the bound alone decides.
A program may use at most 128 MiB of HBM per device.

v0:
```python
import functools

import jax
import jax.numpy as jnp
from jax import lax
from jax.experimental import pallas as pl
from jax.experimental.pallas import tpu as pltpu
from jax.sharding import PartitionSpec as P

epsilon = 1e-05
off_weight = 0.0051
LANES = 128
SUBLANES = 8
HALVES = 2
PARTS = 4
BLOCK = 256
MESH = pl.DeviceIdType.MESH


def split(block):
    high = block.astype(jnp.bfloat16)
    return high, (block - high.astype(jnp.float32)).astype(jnp.bfloat16)


def dot3(left_high, left_low, right_high, right_low, contract):
    def one(left, right):
        return lax.dot_general(
            left, right, (contract, ((), ())), preferred_element_type=jnp.float32
        )

    cross = one(left_high, right_low) + one(left_low, right_high)
    return cross + one(left_high, right_high)


def kernel(
    groups,
    row_devices,
    view_a,
    view_b,
    ga_out,
    gb_out,
    totals_out,
    ends_out,
    a_high,
    a_low,
    at_high,
    at_low,
    raw,
    own_raw,
    ga,
    back_in,
    swap_in,
    pen,
    share_send,
    share_kept,
    share_in,
    block_high,
    block_low,
    pen_high,
    pen_low,
    stats,
    sums,
    sums_in,
    swap_send_sem,
    swap_recv_sem,
    hop_send_sem,
    hop_recv_sem,
    back_send_sem,
    back_recv_sem,
    home_send_sem,
    home_recv_sem,
    share_send_sem,
    share_recv_sem,
    pen_send_sem,
    pen_recv_sem,
    stat_sem,
    sums_send_sem,
    sums_recv_sem,
    load_sem,
    store_sem,
):
    rows, width = a_high.shape
    chunks = width // LANES
    own_jobs = chunks // 2
    jobs = own_jobs + chunks
    bits = row_devices.bit_length() - 1
    slots = bits + 1
    batch = rows * row_devices
    pair = 2 * LANES
    half_rows = rows // HALVES
    part_rows = rows // PARTS

    group = lax.axis_index("grp")
    row = lax.axis_index("row")
    sign = 1 - 2 * lax.rem(group, 2)
    near = (group + sign, row)
    ahead = (lax.rem(group + groups + 2 * sign, groups), row)
    behind = (lax.rem(group + groups - 2 * sign, groups), row)
    digit = [lax.rem(lax.div(row, 1 << b), 2) for b in range(bits)]
    peer = [(group, row + (1 - 2 * digit[b]) * (1 << b)) for b in range(bits)]
    size = [width >> (b + 1) for b in range(bits)]
    start = [0]
    for b in range(bits):
        start.append(start[b] + digit[b] * size[b])
    away = [start[b] + (1 - digit[b]) * size[b] for b in range(bits)]
    share = size[-1]

    barrier = pltpu.get_barrier_semaphore()
    for device in [near, ahead, behind] + peer:
        pl.semaphore_signal(barrier, inc=1, device_id=device, device_id_type=MESH)
    pl.semaphore_wait(barrier, 3 + bits)

    def remote(source, target, send, recv, device):
        return pltpu.make_async_remote_copy(
            src_ref=source,
            dst_ref=target,
            send_sem=send,
            recv_sem=recv,
            device_id=device,
            device_id_type=MESH,
        )

    def lanes_of(chunk):
        return pl.ds(pl.multiple_of(chunk * LANES, LANES), LANES)

    def swap_copy(chunk, half):
        at = pl.ds(half * half_rows, half_rows)
        return remote(
            view_b.at[at, lanes_of(chunk)],
            raw.at[chunks + chunk, at, :],
            swap_send_sem.at[chunk, half],
            swap_recv_sem.at[chunk, half],
            near,
        )

    def hop_copy(chunk, half):
        at = pl.ds(half * half_rows, half_rows)
        return remote(
            raw.at[chunks + chunk, at, :],
            raw.at[2 * chunks + chunk, at, :],
            hop_send_sem.at[chunk, half],
            hop_recv_sem.at[chunk, half],
            ahead,
        )

    def back_copy(chunk, part):
        at = pl.ds(pl.multiple_of(part * part_rows, part_rows), part_rows)
        return remote(
            raw.at[2 * chunks + chunk, at, :],
            back_in.at[chunk, at, :],
            back_send_sem.at[chunk, part],
            back_recv_sem.at[chunk, part],
            behind,
        )

    def home_copy(chunk, part):
        at = pl.ds(pl.multiple_of(part * part_rows, part_rows), part_rows)
        return remote(
            raw.at[chunks + chunk, at, :],
            swap_in.at[chunk, at, :],
            home_send_sem.at[chunk, part],
            home_recv_sem.at[chunk, part],
            near,
        )

    def share_copy(job, b):
        if b == 0:
            source = share_send.at[lax.rem(job, 2)]
        else:
            at = pl.ds(pl.multiple_of(away[b] - start[b], size[b]), size[b])
            source = share_in[b - 1].at[lax.rem(job, slots), at, :]
        return remote(
            source,
            share_in[b].at[lax.rem(job, slots)],
            share_send_sem.at[b, job],
            share_recv_sem.at[b, job],
            peer[b],
        )

    def pen_copy(job, b):
        at = pl.ds(pl.multiple_of(start[b + 1], size[b]), size[b])
        return remote(
            pen.at[lax.rem(job, slots), at, :],
            pen.at[lax.rem(job, slots), at, :],
            pen_send_sem.at[b, job],
            pen_recv_sem.at[b, job],
            peer[b],
        )

    def sums_copy(which, b):
        return remote(
            sums.at[which, b],
            sums_in.at[which, b],
            sums_send_sem.at[which, b],
            sums_recv_sem.at[which, b],
            peer[b],
        )

    def all_sums(which, between):
        for b in range(bits):
            sums_copy(which, b).start()
            between(b)
            sums_copy(which, b).wait()
            sums[which, b + 1] = sums[which, b] + sums_in[which, b]
        return sums[which, bits]

    def stat_near():
        return remote(
            stats.at[pl.ds(0, chunks)],
            stats.at[pl.ds(chunks, chunks)],
            stat_sem.at[0],
            stat_sem.at[1],
            near,
        )

    def stat_ahead():
        return remote(
            stats.at[pl.ds(chunks, chunks)],
            stats.at[pl.ds(2 * chunks, chunks)],
            stat_sem.at[2],
            stat_sem.at[3],
            ahead,
        )

    load_a = pltpu.make_async_copy(view_a, ga, load_sem.at[0])
    load_a.start()

    def load_own(chunk):
        return pltpu.make_async_copy(
            view_b.at[:, lanes_of(chunk)], own_raw.at[chunk], load_sem.at[1 + chunk]
        )

    for chunk in range(chunks):
        load_own(chunk).start()
    for chunk in range(chunks):
        for half in range(HALVES):
            swap_copy(chunk, half).start()
    load_a.wait()

    def folded(block):
        return jnp.sum(block.reshape(-1, SUBLANES, block.shape[-1]), axis=0)

    def add_a(step, carry):
        at = pl.ds(pl.multiple_of(step * LANES, LANES), LANES)
        block = ga[at, :]
        return carry[0] + folded(block), carry[1] + folded(block * block)

    zero = jnp.zeros((SUBLANES, width), jnp.float32)
    first, second = lax.fori_loop(0, rows // LANES, add_a, (zero, zero))
    sums[0, 0] = zero
    sums[0, 0, 0:1, :] = jnp.sum(first, axis=0, keepdims=True)
    sums[0, 0, 1:2, :] = jnp.sum(second, axis=0, keepdims=True)
    for chunk in range(chunks):
        load_own(chunk).wait()
        block = own_raw[chunk]
        raw[chunk] = block
        at = pl.ds(chunk * LANES, LANES)
        sums[0, 0, 2:3, at] = jnp.sum(folded(block), axis=0, keepdims=True)
        sums[0, 0, 3:4, at] = jnp.sum(folded(block * block), axis=0, keepdims=True)

    def relay(chunk, half):
        swap_copy(chunk, half).wait_recv()
        hop_copy(chunk, half).start()

    totals = all_sums(0, lambda b: None)
    totals_out[...] = totals

    def mean_and_inverse(total, square):
        mean = total / batch
        scale = jnp.sqrt(square / batch - mean * mean + epsilon)
        return mean, 1.0 / scale

    mean_a, inverse_a = mean_and_inverse(totals[0:1, :], totals[1:2, :])
    mean_b, inverse_b = mean_and_inverse(totals[2:3, :], totals[3:4, :])
    for chunk in range(chunks):
        at = slice(chunk * LANES, (chunk + 1) * LANES)
        stats[chunk] = jnp.zeros((SUBLANES, LANES), jnp.float32)
        stats[chunk, 0:1, :] = mean_b[:, at]
        stats[chunk, 1:2, :] = inverse_b[:, at]
    stat_near().start()

    def norm_a(step, carry):
        at = pl.ds(pl.multiple_of(step * LANES, LANES), LANES)
        block = (ga[at, :] - mean_a) * inverse_a
        a_high[at, :], a_low[at, :] = split(block)
        at_high[:, at], at_low[:, at] = split(block.T)
        ga[at, :] = jnp.zeros_like(block)
        return carry

    lax.fori_loop(0, rows // LANES // 2, norm_a, 0)
    relay(0, 0)
    lax.fori_loop(rows // LANES // 2, rows // LANES, norm_a, 0)
    stat_near().wait_recv()
    stat_ahead().start()
    for half in range(1, HALVES):
        relay(0, half)

    def places(job):
        is_own = job < own_jobs
        chunk = job - own_jobs
        first = jnp.where(is_own, 2 * job, chunks + chunk)
        second = jnp.where(is_own, 2 * job + 1, 2 * chunks + chunk)
        return first, second

    def load_block(job):
        for part, place in enumerate(places(job)):
            mean = stats[place, 0:1, :]
            inverse = stats[place, 1:2, :]
            high, low = split((raw[place] - mean) * inverse)
            at = slice(part * LANES, (part + 1) * LANES)
            block_high[:, at] = high
            block_low[:, at] = low

    def correlate(job):
        @pl.when(job >= own_jobs)
        def _():
            @pl.when(job == own_jobs)
            def _():
                stat_ahead().wait_recv()

            for half in range(HALVES):
                hop_copy(job - own_jobs, half).wait_recv()

        load_block(job)

        def part_of(target, base):
            count = min(BLOCK, size[0])

            def body(step, carry):
                offset = pl.multiple_of(step * count, count)
                at = pl.ds(pl.multiple_of(base + offset, count), count)
                target[pl.ds(offset, count), :] = dot3(
                    at_high[at, :],
                    at_low[at, :],
                    block_high[...],
                    block_low[...],
                    ((1,), (0,)),
                ) * (1.0 / batch)
                return carry

            lax.fori_loop(0, size[0] // count, body, 0)

        part_of(share_send.at[lax.rem(job, 2)], away[0])
        share_copy(job, 0).start()
        part_of(share_kept, start[1])

    def reduce_step(job, b):
        share_copy(job, b).wait()
        slot = lax.rem(job, slots)
        if b == 0:
            kept = share_kept[...]
        else:
            at = pl.ds(pl.multiple_of(start[b + 1] - start[b], size[b]), size[b])
            kept = share_in[b - 1][slot, at, :]
        total = kept + share_in[b][slot]
        if b < bits - 1:
            share_in[b][slot] = total
            share_copy(job, b + 1).start()
            return
        shape = (share, pair)
        row_index = start[bits] + lax.broadcasted_iota(jnp.int32, shape, 0)
        base = jnp.where(job < own_jobs, job * pair, -width)
        column = base + lax.broadcasted_iota(jnp.int32, shape, 1)
        value = jnp.where(
            column == row_index, -2.0 * (1.0 - total), 2.0 * off_weight * total
        )
        at = pl.ds(pl.multiple_of(start[bits], share), share)
        pen[slot, at, :] = value
        pen_copy(job, bits - 1).start()

    def gather_step(job, b):
        pen_copy(job, b).wait()
        pen_copy(job, b - 1).start()

    def consume(job):
        pen_copy(job, 0).wait()
        slot = lax.rem(job, slots)
        pen_high[...], pen_low[...] = split(pen[slot])
        load_block(job)
        first, second = places(job)

        @pl.when(job >= own_jobs)
        def _():
            for half in range(HALVES):
                hop_copy(job - own_jobs, half).wait_send()

        def contribute(step, carry):
            at = pl.ds(pl.multiple_of(step * BLOCK, BLOCK), BLOCK)
            value = dot3(
                a_high[at, :], a_low[at, :], pen_high[...], pen_low[...], ((1,), (0,))
            )
            raw[first, at, :] = value[:, :LANES]
            raw[second, at, :] = value[:, LANES:]
            return carry

        lax.fori_loop(0, rows // BLOCK, contribute, 0)

        @pl.when(job >= own_jobs)
        def _():
            for part in range(PARTS):
                back_copy(job - own_jobs, part).start()

        def accumulate(step, carry):
            at = pl.ds(pl.multiple_of(step * BLOCK, BLOCK), BLOCK)
            ga[at, :] += dot3(
                block_high[at, :],
                block_low[at, :],
                pen_high[...],
                pen_low[...],
                ((1,), (1,)),
            )
            return carry

        lax.fori_loop(0, rows // BLOCK, accumulate, 0)

    def step_of(job, k):
        if k <= bits:
            reduce_step(job, k - 1)
        else:
            gather_step(job, 2 * bits - k)

    def send_home(chunk):
        def body(part, carry):
            back_copy(chunk, part).wait_recv()
            at = pl.ds(pl.multiple_of(part * part_rows, part_rows), part_rows)
            raw[chunks + chunk, at, :] += back_in[chunk, at, :]
            home_copy(chunk, part).start()
            return carry

        lax.fori_loop(0, PARTS, body, 0)

    def tick(t, carry):
        following = t - own_jobs + 1
        relays = jnp.logical_and(following >= 1, following < chunks)

        @pl.when(relays)
        def _():
            relay(following, 0)

        def run(job, action):
            pl.when(jnp.logical_and(job >= 0, job < jobs))(lambda: action(job))

        for k in range(2 * bits - 2, 0, -2):
            run(t - k // 2, functools.partial(step_of, k=k))
        run(t, correlate)

        @pl.when(relays)
        def _():
            for half in range(1, HALVES):
                relay(following, half)

        run(t - bits, consume)
        for k in range(1, 2 * bits, 2):
            run(t - k // 2, functools.partial(step_of, k=k))
        home = t - own_jobs - bits - 1

        @pl.when(jnp.logical_and(home >= 0, home < chunks))
        def _():
            send_home(home)

        return carry

    lax.fori_loop(0, jobs + bits + 1, tick, 0)

    def store_a():
        return pltpu.make_async_copy(ga, ga_out, store_sem.at[0])

    def store_b(chunk):
        return pltpu.make_async_copy(
            raw.at[chunk], gb_out.at[:, lanes_of(chunk)], store_sem.at[1 + chunk]
        )

    store_a().start()

    def end_a(step, carry):
        at = pl.ds(pl.multiple_of(step * LANES, LANES), LANES)
        block = ga[at, :]
        normed = a_high[at, :].astype(jnp.float32) + a_low[at, :].astype(jnp.float32)
        return carry[0] + folded(block), carry[1] + folded(block * normed)

    first, second = lax.fori_loop(0, rows // LANES, end_a, (zero, zero))
    sums[1, 0] = zero
    sums[1, 0, 0:1, :] = jnp.sum(first, axis=0, keepdims=True)
    sums[1, 0, 1:2, :] = jnp.sum(second, axis=0, keepdims=True)
    for chunk in range(chunks):
        mean = stats[chunk, 0:1, :]
        inverse = stats[chunk, 1:2, :]

        def end_b(part, carry):
            home_copy(chunk, part).wait_recv()
            at = pl.ds(pl.multiple_of(part * part_rows, part_rows), part_rows)
            block = raw[chunk, at, :] + swap_in[chunk, at, :]
            raw[chunk, at, :] = block
            normed = (own_raw[chunk, at, :] - mean) * inverse
            return carry[0] + folded(block), carry[1] + folded(block * normed)

        small = jnp.zeros((SUBLANES, LANES), jnp.float32)
        first, second = lax.fori_loop(0, PARTS, end_b, (small, small))
        store_b(chunk).start()
        at = pl.ds(chunk * LANES, LANES)
        sums[1, 0, 2:3, at] = jnp.sum(first, axis=0, keepdims=True)
        sums[1, 0, 3:4, at] = jnp.sum(second, axis=0, keepdims=True)
    ends_out[...] = all_sums(1, lambda b: None)

    stat_near().wait_send()
    stat_ahead().wait_send()

    def drain(chunk, carry):
        for half in range(HALVES):
            swap_copy(chunk, half).wait_send()
        for part in range(PARTS):
            back_copy(chunk, part).wait_send()
            home_copy(chunk, part).wait_send()
        store_b(chunk).wait()
        return carry

    lax.fori_loop(0, chunks, drain, 0)
    store_a().wait()


def per_device(view_a, view_b):
    rows, width = view_a.shape
    row_devices = lax.axis_size("row")
    groups = lax.axis_size("grp")
    batch = rows * row_devices
    bits = row_devices.bit_length() - 1
    chunks = width // LANES
    jobs = chunks // 2 + chunks
    slots = bits + 1
    pair = 2 * LANES
    f32, bf16 = jnp.float32, jnp.bfloat16
    dma = pltpu.SemaphoreType.DMA
    large = jax.ShapeDtypeStruct((rows, width), f32)
    small = jax.ShapeDtypeStruct((SUBLANES, width), f32)
    anywhere = pl.BlockSpec(memory_space=pl.ANY)
    vmem = pl.BlockSpec(memory_space=pltpu.VMEM)
    grad_a, grad_b, totals, ends = pl.pallas_call(
        functools.partial(kernel, groups, row_devices),
        out_shape=[large, large, small, small],
        in_specs=[anywhere, anywhere],
        out_specs=[anywhere, anywhere, vmem, vmem],
        scratch_shapes=[
            pltpu.VMEM((rows, width), bf16),
            pltpu.VMEM((rows, width), bf16),
            pltpu.VMEM((width, rows), bf16),
            pltpu.VMEM((width, rows), bf16),
            pltpu.VMEM((3 * chunks, rows, LANES), f32),
            pltpu.VMEM((chunks, rows, LANES), f32),
            pltpu.VMEM((rows, width), f32),
            pltpu.VMEM((chunks, rows, LANES), f32),
            pltpu.VMEM((chunks, rows, LANES), f32),
            pltpu.VMEM((slots, width, pair), f32),
            pltpu.VMEM((2, width // 2, pair), f32),
            pltpu.VMEM((width // 2, pair), f32),
            [pltpu.VMEM((slots, width >> (b + 1), pair), f32) for b in range(bits)],
            pltpu.VMEM((rows, pair), bf16),
            pltpu.VMEM((rows, pair), bf16),
            pltpu.VMEM((width, pair), bf16),
            pltpu.VMEM((width, pair), bf16),
            pltpu.VMEM((3 * chunks, SUBLANES, LANES), f32),
            pltpu.VMEM((2, bits + 1, SUBLANES, width), f32),
            pltpu.VMEM((2, bits, SUBLANES, width), f32),
            dma((chunks, HALVES)),
            dma((chunks, HALVES)),
            dma((chunks, HALVES)),
            dma((chunks, HALVES)),
            dma((chunks, PARTS)),
            dma((chunks, PARTS)),
            dma((chunks, PARTS)),
            dma((chunks, PARTS)),
            dma((bits, jobs)),
            dma((bits, jobs)),
            dma((bits, jobs)),
            dma((bits, jobs)),
            dma((4,)),
            dma((2, bits)),
            dma((2, bits)),
            dma((1 + chunks,)),
            dma((1 + chunks,)),
        ],
        compiler_params=pltpu.CompilerParams(
            collective_id=0, has_side_effects=True, vmem_limit_bytes=66_000_000
        ),
        name="twins",
    )(view_a, view_b)

    def finish(grad, view, total, square, end, cross):
        mean = total / batch
        scale = jnp.sqrt(square / batch - mean * mean + epsilon)
        normed = (view - mean) / scale
        return (grad - end / batch - normed * (cross / batch)) / scale

    return (
        finish(grad_a, view_a, totals[0], totals[1], ends[0], ends[1]),
        finish(grad_b, view_b, totals[2], totals[3], ends[2], ends[3]),
    )


def solution(mesh):
    placed = (P("row", "grp"), P("row", "grp"))
    return jax.shard_map(
        per_device, mesh=mesh, in_specs=placed, out_specs=placed, check_vma=False
    )
```

profile of v0, /device:TPU:0, one launch (start us, length us, event | category | flops | bytes accessed | tf_op | source)
XLA Modules:
  0.0 352.3 jit_solution(11506481086695531605)
XLA Ops:
  0.6 340.4 %twins.1 = (f32[1024,1024]{1,0:T(8,128)}, f32[1024,1024]{1,0:T(8,128)}, f32[8,1024]{1,0:T(8,128)}, f32[8,1024]{1,0:T(8,128)}) custom-call(f32[1024,1024]{1,0:T(8,128)} %view_a.1, f32[1024,1024]{1,0:T(8,128)} %view_b.1), custom_call_target="tpu_custom_call" | custom-call | tf_op jit(solution)/shard_map/twins/pallas_call | solution.py:537
  341.0 0.9 slice_multiply_fusion.2
  341.9 0.9 slice_multiply_fusion.1
  342.9 9.5 %subtract_divide_fusion = (f32[1024,1024]{1,0:T(8,128)}, f32[1024,1024]{1,0:T(8,128)}) fusion(f32[1024,1024]{1,0:T(8,128)} %view_b.1, f32[1024,1024]{1,0:T(8,128)} %get-tuple-element.9, f32[1024]{0:T(1024)S(1)} %bitcast.9, f32[1024]{0:T(1024)S(1)} %bitcast.13, f32[1024]{0:T(1024)S(1)} %bitcast.12, f32[1024]{0:T(1024)S(1)} %bitcast.8, f32[1024]{0:T(1024)S(1)} %bitcast.10, ...), kind=kLoop, calls=%fused_computation | loop fusion | flops 12582912 | bytes 25198592 | tf_op jit(solution)/shard_map/div | solution.py:591
where the time goes:
time: 353 us; the launch traced here: 352 us
  Pallas kernels  340 us (96%)
  other arithmetic  11.3 us (3%)
    pallas_call x1, Pallas kernels, per_device(): pl.pallas_call(functools.partial(kernel, groups, row_devices), out_shape=...  340 us
    div x2, other arithmetic, finish(): return (grad - end / batch - normed * (cross / batch)) / scale  10.4 us

commit v1 on v0

--- a/solution.py
+++ b/solution.py
@@ -11,9 +11,11 @@
 off_weight = 0.0051
 LANES = 128
 SUBLANES = 8
-HALVES = 2
+HALVES = 1
 PARTS = 4
 BLOCK = 256
+WINDOW = 1
+HOLD = 2
 MESH = pl.DeviceIdType.MESH
 
 
@@ -84,7 +86,9 @@
     own_jobs = chunks // 2
     jobs = own_jobs + chunks
     bits = row_devices.bit_length() - 1
-    slots = bits + 1
+    slots = 2 * bits
+    delay = 2 * bits - 1
+    hold = max(chunks - HOLD, delay + 1)
     batch = rows * row_devices
     pair = 2 * LANES
     half_rows = rows // HALVES
@@ -222,6 +226,9 @@
             ahead,
         )
 
+    for chunk in range(min(WINDOW, chunks)):
+        for half in range(HALVES):
+            swap_copy(chunk, half).start()
     load_a = pltpu.make_async_copy(view_a, ga, load_sem.at[0])
     load_a.start()
 
@@ -232,9 +239,6 @@
 
     for chunk in range(chunks):
         load_own(chunk).start()
-    for chunk in range(chunks):
-        for half in range(HALVES):
-            swap_copy(chunk, half).start()
     load_a.wait()
 
     def folded(block):
@@ -246,6 +250,14 @@
         return carry[0] + folded(block), carry[1] + folded(block * block)
 
     zero = jnp.zeros((SUBLANES, width), jnp.float32)
+    def relay(chunk, half):
+        swap_copy(chunk, half).wait_recv()
+        hop_copy(chunk, half).start()
+
+        @pl.when(chunk + WINDOW < chunks)
+        def _():
+            swap_copy(chunk + WINDOW, half).start()
+
     first, second = lax.fori_loop(0, rows // LANES, add_a, (zero, zero))
     sums[0, 0] = zero
     sums[0, 0, 0:1, :] = jnp.sum(first, axis=0, keepdims=True)
@@ -258,11 +270,8 @@
         sums[0, 0, 2:3, at] = jnp.sum(folded(block), axis=0, keepdims=True)
         sums[0, 0, 3:4, at] = jnp.sum(folded(block * block), axis=0, keepdims=True)
 
-    def relay(chunk, half):
-        swap_copy(chunk, half).wait_recv()
-        hop_copy(chunk, half).start()
-
     totals = all_sums(0, lambda b: None)
+    relay(0, 0)
     totals_out[...] = totals
 
     def mean_and_inverse(total, square):
@@ -288,19 +297,21 @@
         return carry
 
     lax.fori_loop(0, rows // LANES // 2, norm_a, 0)
-    relay(0, 0)
     lax.fori_loop(rows // LANES // 2, rows // LANES, norm_a, 0)
     stat_near().wait_recv()
     stat_ahead().start()
-    for half in range(1, HALVES):
-        relay(0, half)
+    def own_of(job):
+        return job >= chunks, job - chunks
 
     def places(job):
-        is_own = job < own_jobs
-        chunk = job - own_jobs
-        first = jnp.where(is_own, 2 * job, chunks + chunk)
-        second = jnp.where(is_own, 2 * job + 1, 2 * chunks + chunk)
+        is_own, index = own_of(job)
+        chunk = job
+        first = jnp.where(is_own, 2 * index, chunks + chunk)
+        second = jnp.where(is_own, 2 * index + 1, 2 * chunks + chunk)
         return first, second
+
+    def when_pair(job, action):
+        pl.when(job < chunks)(lambda: action(job))
 
     def load_block(job):
         for part, place in enumerate(places(job)):
@@ -312,15 +323,15 @@
             block_low[:, at] = low
 
     def correlate(job):
-        @pl.when(job >= own_jobs)
+        @pl.when(job == 0)
         def _():
-            @pl.when(job == own_jobs)
-            def _():
-                stat_ahead().wait_recv()
-
+            stat_ahead().wait_recv()
+
+        def arrived(chunk):
             for half in range(HALVES):
-                hop_copy(job - own_jobs, half).wait_recv()
-
+                hop_copy(chunk, half).wait_recv()
+
+        when_pair(job, arrived)
         load_block(job)
 
         def part_of(target, base):
@@ -359,7 +370,8 @@
             return
         shape = (share, pair)
         row_index = start[bits] + lax.broadcasted_iota(jnp.int32, shape, 0)
-        base = jnp.where(job < own_jobs, job * pair, -width)
+        is_own, index = own_of(job)
+        base = jnp.where(is_own, index * pair, -width)
         column = base + lax.broadcasted_iota(jnp.int32, shape, 1)
         value = jnp.where(
             column == row_index, -2.0 * (1.0 - total), 2.0 * off_weight * total
@@ -379,10 +391,11 @@
         load_block(job)
         first, second = places(job)
 
-        @pl.when(job >= own_jobs)
-        def _():
+        def hopped(chunk):
             for half in range(HALVES):
-                hop_copy(job - own_jobs, half).wait_send()
+                hop_copy(chunk, half).wait_send()
+
+        when_pair(job, hopped)
 
         def contribute(step, carry):
             at = pl.ds(pl.multiple_of(step * BLOCK, BLOCK), BLOCK)
@@ -394,11 +407,6 @@
             return carry
 
         lax.fori_loop(0, rows // BLOCK, contribute, 0)
-
-        @pl.when(job >= own_jobs)
-        def _():
-            for part in range(PARTS):
-                back_copy(job - own_jobs, part).start()
 
         def accumulate(step, carry):
             at = pl.ds(pl.multiple_of(step * BLOCK, BLOCK), BLOCK)
@@ -430,8 +438,8 @@
         lax.fori_loop(0, PARTS, body, 0)
 
     def tick(t, carry):
-        following = t - own_jobs + 1
-        relays = jnp.logical_and(following >= 1, following < chunks)
+        following = t + 1
+        relays = following < chunks
 
         @pl.when(relays)
         def _():
@@ -440,27 +448,21 @@
         def run(job, action):
             pl.when(jnp.logical_and(job >= 0, job < jobs))(lambda: action(job))
 
-        for k in range(2 * bits - 2, 0, -2):
-            run(t - k // 2, functools.partial(step_of, k=k))
+        def send_back(chunk):
+            for part in range(PARTS):
+                back_copy(chunk, part).start()
+
+        turn = t - hold
+        pl.when(jnp.logical_and(turn >= 0, turn < chunks))(lambda: send_back(turn))
+        home = turn - 1
+        pl.when(jnp.logical_and(home >= 0, home < chunks))(lambda: send_home(home))
         run(t, correlate)
-
-        @pl.when(relays)
-        def _():
-            for half in range(1, HALVES):
-                relay(following, half)
-
-        run(t - bits, consume)
-        for k in range(1, 2 * bits, 2):
-            run(t - k // 2, functools.partial(step_of, k=k))
-        home = t - own_jobs - bits - 1
-
-        @pl.when(jnp.logical_and(home >= 0, home < chunks))
-        def _():
-            send_home(home)
-
+        run(t - delay, consume)
+        for k in range(delay, 0, -1):
+            run(t - k + 1, functools.partial(step_of, k=k))
         return carry
 
-    lax.fori_loop(0, jobs + bits + 1, tick, 0)
+    lax.fori_loop(0, max(jobs + delay, hold + chunks + 1), tick, 0)
 
     def store_a():
         return pltpu.make_async_copy(ga, ga_out, store_sem.at[0])
@@ -526,7 +528,7 @@
     bits = row_devices.bit_length() - 1
     chunks = width // LANES
     jobs = chunks // 2 + chunks
-    slots = bits + 1
+    slots = 2 * bits
     pair = 2 * LANES
     f32, bf16 = jnp.float32, jnp.bfloat16
     dma = pltpu.SemaphoreType.DMA

time: 353 us -> 232 us (0.66)
  Pallas kernels: 340 us -> 220 us
    pallas_call x1, Pallas kernels: 340 us -> 220 us  [per_device(): pl.pallas_call(functools.partial(kernel, groups, row_devices), out_shape=...]
where the time goes in v1:
time: 232 us
  Pallas kernels  220 us (95%)
  other arithmetic  11.3 us (5%)
    pallas_call x1, Pallas kernels, per_device(): pl.pallas_call(functools.partial(kernel, groups, row_devices), out_shape=...  220 us
    div x2, other arithmetic, finish(): return (grad - end / batch - normed * (cross / batch)) / scale  10.4 us

profile of v1, /device:TPU:0, one launch (start us, length us, event | category | flops | bytes accessed | tf_op | source)
XLA Modules:
  0.0 231.9 jit_solution(4621100916247551900)
XLA Ops:
  0.6 219.9 %twins.1 = (f32[1024,1024]{1,0:T(8,128)}, f32[1024,1024]{1,0:T(8,128)}, f32[8,1024]{1,0:T(8,128)}, f32[8,1024]{1,0:T(8,128)}) custom-call(f32[1024,1024]{1,0:T(8,128)} %view_a.1, f32[1024,1024]{1,0:T(8,128)} %view_b.1), custom_call_target="tpu_custom_call" | custom-call | tf_op jit(solution)/shard_map/twins/pallas_call | solution.py:539
  220.6 0.9 slice_multiply_fusion.2
  221.5 0.9 slice_multiply_fusion.1
  222.4 9.5 %subtract_divide_fusion = (f32[1024,1024]{1,0:T(8,128)}, f32[1024,1024]{1,0:T(8,128)}) fusion(f32[1024,1024]{1,0:T(8,128)} %view_b.1, f32[1024,1024]{1,0:T(8,128)} %get-tuple-element.9, f32[1024]{0:T(1024)S(1)} %bitcast.9, f32[1024]{0:T(1024)S(1)} %bitcast.13, f32[1024]{0:T(1024)S(1)} %bitcast.12, f32[1024]{0:T(1024)S(1)} %bitcast.8, f32[1024]{0:T(1024)S(1)} %bitcast.10, ...), kind=kLoop, calls=%fused_computation | loop fusion | flops 12582912 | bytes 25198592 | tf_op jit(solution)/shard_map/div | solution.py:593

commit v2 on v1

--- a/solution.py
+++ b/solution.py
@@ -12,10 +12,13 @@
 LANES = 128
 SUBLANES = 8
 HALVES = 1
-PARTS = 4
+PARTS = 2
 BLOCK = 256
+VMEM_LIMIT = 50 << 20
+HOLD = 2
 WINDOW = 1
-HOLD = 2
+BACK_AT = 2
+HOME_AT = 3
 MESH = pl.DeviceIdType.MESH
 
 
@@ -39,17 +42,14 @@
     row_devices,
     view_a,
     view_b,
-    ga_out,
+    ga,
     gb_out,
-    totals_out,
-    ends_out,
     a_high,
     a_low,
     at_high,
     at_low,
     raw,
     own_raw,
-    ga,
     back_in,
     swap_in,
     pen,
@@ -79,7 +79,6 @@
     sums_send_sem,
     sums_recv_sem,
     load_sem,
-    store_sem,
 ):
     rows, width = a_high.shape
     chunks = width // LANES
@@ -200,10 +199,9 @@
             peer[b],
         )
 
-    def all_sums(which, between):
+    def all_sums(which):
         for b in range(bits):
             sums_copy(which, b).start()
-            between(b)
             sums_copy(which, b).wait()
             sums[which, b + 1] = sums[which, b] + sums_in[which, b]
         return sums[which, bits]
@@ -226,9 +224,7 @@
             ahead,
         )
 
-    for chunk in range(min(WINDOW, chunks)):
-        for half in range(HALVES):
-            swap_copy(chunk, half).start()
+    swap_copy(0, 0).start()
     load_a = pltpu.make_async_copy(view_a, ga, load_sem.at[0])
     load_a.start()
 
@@ -240,6 +236,8 @@
     for chunk in range(chunks):
         load_own(chunk).start()
     load_a.wait()
+    for half in range(1, HALVES):
+        swap_copy(0, half).start()
 
     def folded(block):
         return jnp.sum(block.reshape(-1, SUBLANES, block.shape[-1]), axis=0)
@@ -270,9 +268,13 @@
         sums[0, 0, 2:3, at] = jnp.sum(folded(block), axis=0, keepdims=True)
         sums[0, 0, 3:4, at] = jnp.sum(folded(block * block), axis=0, keepdims=True)
 
-    totals = all_sums(0, lambda b: None)
+    for chunk in range(1, WINDOW):
+        for half in range(HALVES):
+            swap_copy(chunk, half).start()
     relay(0, 0)
-    totals_out[...] = totals
+    totals = all_sums(0)
+    for half in range(1, HALVES):
+        relay(0, half)
 
     def mean_and_inverse(total, square):
         mean = total / batch
@@ -448,61 +450,116 @@
         def run(job, action):
             pl.when(jnp.logical_and(job >= 0, job < jobs))(lambda: action(job))
 
-        def send_back(chunk):
-            for part in range(PARTS):
-                back_copy(chunk, part).start()
-
         turn = t - hold
-        pl.when(jnp.logical_and(turn >= 0, turn < chunks))(lambda: send_back(turn))
+
+        def send_back(first, last):
+            for part in range(first, last):
+                back_copy(turn, part).start()
+
+        inside = jnp.logical_and(turn >= 0, turn < chunks)
         home = turn - 1
-        pl.when(jnp.logical_and(home >= 0, home < chunks))(lambda: send_home(home))
+        sent = jnp.logical_and(home >= 0, home < chunks - 1)
+
+        def backs(place):
+            if place == BACK_AT:
+                pl.when(inside)(lambda: send_back(0, PARTS))
+
+        def homes(place):
+            if place == HOME_AT:
+                pl.when(sent)(lambda: send_home(home))
+
+        backs(0)
+        homes(0)
         run(t, correlate)
+        backs(1)
+        homes(1)
+
+        @pl.when(relays)
+        def _():
+            for half in range(1, HALVES):
+                relay(following, half)
+
         run(t - delay, consume)
+        backs(2)
+        homes(2)
         for k in range(delay, 0, -1):
             run(t - k + 1, functools.partial(step_of, k=k))
+        backs(3)
+        homes(3)
         return carry
 
-    lax.fori_loop(0, max(jobs + delay, hold + chunks + 1), tick, 0)
-
-    def store_a():
-        return pltpu.make_async_copy(ga, ga_out, store_sem.at[0])
-
-    def store_b(chunk):
-        return pltpu.make_async_copy(
-            raw.at[chunk], gb_out.at[:, lanes_of(chunk)], store_sem.at[1 + chunk]
-        )
-
-    store_a().start()
+    lax.fori_loop(0, max(jobs + delay, hold + chunks), tick, 0)
 
     def end_a(step, carry):
         at = pl.ds(pl.multiple_of(step * LANES, LANES), LANES)
         block = ga[at, :]
-        normed = a_high[at, :].astype(jnp.float32) + a_low[at, :].astype(jnp.float32)
-        return carry[0] + folded(block), carry[1] + folded(block * normed)
+        return carry[0] + folded(block), carry[1] + folded(block * normed_a(at))
+
+    def normed_a(at):
+        return a_high[at, :].astype(jnp.float32) + a_low[at, :].astype(jnp.float32)
 
     first, second = lax.fori_loop(0, rows // LANES, end_a, (zero, zero))
     sums[1, 0] = zero
     sums[1, 0, 0:1, :] = jnp.sum(first, axis=0, keepdims=True)
     sums[1, 0, 1:2, :] = jnp.sum(second, axis=0, keepdims=True)
-    for chunk in range(chunks):
+    sums_copy(1, 0).start()
+    sums[2, 0] = zero
+
+    def normed_b(chunk, at):
         mean = stats[chunk, 0:1, :]
-        inverse = stats[chunk, 1:2, :]
-
-        def end_b(part, carry):
+        return (own_raw[chunk, at, :] - mean) * stats[chunk, 1:2, :]
+
+    def end_b(chunk):
+        def body(part, carry):
             home_copy(chunk, part).wait_recv()
             at = pl.ds(pl.multiple_of(part * part_rows, part_rows), part_rows)
             block = raw[chunk, at, :] + swap_in[chunk, at, :]
             raw[chunk, at, :] = block
-            normed = (own_raw[chunk, at, :] - mean) * inverse
-            return carry[0] + folded(block), carry[1] + folded(block * normed)
+            cross = folded(block * normed_b(chunk, at))
+            return carry[0] + folded(block), carry[1] + cross
 
         small = jnp.zeros((SUBLANES, LANES), jnp.float32)
-        first, second = lax.fori_loop(0, PARTS, end_b, (small, small))
-        store_b(chunk).start()
+        first, second = lax.fori_loop(0, PARTS, body, (small, small))
         at = pl.ds(chunk * LANES, LANES)
-        sums[1, 0, 2:3, at] = jnp.sum(first, axis=0, keepdims=True)
-        sums[1, 0, 3:4, at] = jnp.sum(second, axis=0, keepdims=True)
-    ends_out[...] = all_sums(1, lambda b: None)
+        sums[2, 0, 0:1, at] = jnp.sum(first, axis=0, keepdims=True)
+        sums[2, 0, 1:2, at] = jnp.sum(second, axis=0, keepdims=True)
+
+    for chunk in range(chunks - 2):
+        end_b(chunk)
+    send_home(chunks - 1)
+    for b in range(bits):
+        if b > 0:
+            sums_copy(1, b).start()
+        sums_copy(1, b).wait()
+        sums[1, b + 1] = sums[1, b] + sums_in[1, b]
+    ends = sums[1, bits] / batch
+    end_mean, end_cross = ends[0:1, :], ends[1:2, :]
+
+    def finish_a(step, carry):
+        at = pl.ds(pl.multiple_of(step * LANES, LANES), LANES)
+        ga[at, :] = (ga[at, :] - end_mean - normed_a(at) * end_cross) * inverse_a
+        return carry
+
+    lax.fori_loop(0, rows // LANES, finish_a, 0)
+    for chunk in range(chunks - 2, chunks):
+        end_b(chunk)
+    for b in range(bits):
+        sums_copy(2, b).start()
+        sums_copy(2, b).wait()
+        sums[2, b + 1] = sums[2, b] + sums_in[2, b]
+    for chunk in range(chunks):
+        at = pl.ds(chunk * LANES, LANES)
+        end_mean = sums[2, bits, 0:1, at] / batch
+        end_cross = sums[2, bits, 1:2, at] / batch
+        inverse = stats[chunk, 1:2, :]
+
+        def finish_b(part, carry):
+            here = pl.ds(pl.multiple_of(part * part_rows, part_rows), part_rows)
+            removed = end_mean + normed_b(chunk, here) * end_cross
+            gb_out[here, at] = (raw[chunk, here, :] - removed) * inverse
+            return carry
+
+        lax.fori_loop(0, PARTS, finish_b, 0)
 
     stat_near().wait_send()
     stat_ahead().wait_send()
@@ -513,18 +570,15 @@
         for part in range(PARTS):
             back_copy(chunk, part).wait_send()
             home_copy(chunk, part).wait_send()
-        store_b(chunk).wait()
         return carry
 
     lax.fori_loop(0, chunks, drain, 0)
-    store_a().wait()
 
 
 def per_device(view_a, view_b):
     rows, width = view_a.shape
     row_devices = lax.axis_size("row")
     groups = lax.axis_size("grp")
-    batch = rows * row_devices
     bits = row_devices.bit_length() - 1
     chunks = width // LANES
     jobs = chunks // 2 + chunks
@@ -532,15 +586,13 @@
     pair = 2 * LANES
     f32, bf16 = jnp.float32, jnp.bfloat16
     dma = pltpu.SemaphoreType.DMA
-    large = jax.ShapeDtypeStruct((rows, width), f32)
-    small = jax.ShapeDtypeStruct((SUBLANES, width), f32)
     anywhere = pl.BlockSpec(memory_space=pl.ANY)
     vmem = pl.BlockSpec(memory_space=pltpu.VMEM)
-    grad_a, grad_b, totals, ends = pl.pallas_call(
+    grad_a, grad_b = pl.pallas_call(
         functools.partial(kernel, groups, row_devices),
-        out_shape=[large, large, small, small],
+        out_shape=[pltpu.VMEM((rows, width), f32)] * 2,
         in_specs=[anywhere, anywhere],
-        out_specs=[anywhere, anywhere, vmem, vmem],
+        out_specs=[vmem, vmem],
         scratch_shapes=[
             pltpu.VMEM((rows, width), bf16),
             pltpu.VMEM((rows, width), bf16),
@@ -548,7 +600,6 @@
             pltpu.VMEM((width, rows), bf16),
             pltpu.VMEM((3 * chunks, rows, LANES), f32),
             pltpu.VMEM((chunks, rows, LANES), f32),
-            pltpu.VMEM((rows, width), f32),
             pltpu.VMEM((chunks, rows, LANES), f32),
             pltpu.VMEM((chunks, rows, LANES), f32),
             pltpu.VMEM((slots, width, pair), f32),
@@ -560,8 +611,8 @@
             pltpu.VMEM((width, pair), bf16),
             pltpu.VMEM((width, pair), bf16),
             pltpu.VMEM((3 * chunks, SUBLANES, LANES), f32),
-            pltpu.VMEM((2, bits + 1, SUBLANES, width), f32),
-            pltpu.VMEM((2, bits, SUBLANES, width), f32),
+            pltpu.VMEM((3, bits + 1, SUBLANES, width), f32),
+            pltpu.VMEM((3, bits, SUBLANES, width), f32),
             dma((chunks, HALVES)),
             dma((chunks, HALVES)),
             dma((chunks, HALVES)),
@@ -575,27 +626,17 @@
             dma((bits, jobs)),
             dma((bits, jobs)),
             dma((4,)),
-            dma((2, bits)),
-            dma((2, bits)),
-            dma((1 + chunks,)),
+            dma((3, bits)),
+            dma((3, bits)),
             dma((1 + chunks,)),
         ],
         compiler_params=pltpu.CompilerParams(
-            collective_id=0, has_side_effects=True, vmem_limit_bytes=66_000_000
+            collective_id=0, has_side_effects=True, vmem_limit_bytes=VMEM_LIMIT
         ),
         name="twins",
     )(view_a, view_b)
 
-    def finish(grad, view, total, square, end, cross):
-        mean = total / batch
-        scale = jnp.sqrt(square / batch - mean * mean + epsilon)
-        normed = (view - mean) / scale
-        return (grad - end / batch - normed * (cross / batch)) / scale
-
-    return (
-        finish(grad_a, view_a, totals[0], totals[1], ends[0], ends[1]),
-        finish(grad_b, view_b, totals[2], totals[3], ends[2], ends[3]),
-    )
+    return grad_a, grad_b
 
 
 def solution(mesh):

time: 232 us -> 223 us (0.961)
  other arithmetic: 11.3 us -> 0 us
  local copies, waits for them, and re-layouts: 0 us -> 4.03 us
    div x3 -> x0, other arithmetic: 11.3 us -> none  [the longest x2 10.4 us: finish(): return (grad - end / batch - normed * (cross / batch)) / scale]
    unnamed x0 -> x2, local copies, waits for them, and re-layouts: none -> 4.03 us
where the time goes in v2:
time: 223 us
  Pallas kernels  218 us (98%)
  local copies, waits for them, and re-layouts  4.03 us (2%)
    pallas_call x1, Pallas kernels, per_device(): pl.pallas_call(functools.partial(kernel, groups, row_devices), out_shape=...  218 us

profile of v2, /device:TPU:0, one launch (start us, length us, event | category | flops | bytes accessed | tf_op | source)
XLA Modules:
  0.0 222.7 jit_solution(5687894805803518112)
XLA Ops:
  0.6 218.0 %twins.1 = (f32[1024,1024]{1,0:T(8,128)S(1)}, f32[1024,1024]{1,0:T(8,128)S(1)}) custom-call(f32[1024,1024]{1,0:T(8,128)} %view_a.1, f32[1024,1024]{1,0:T(8,128)} %view_b.1), custom_call_target="tpu_custom_call" | custom-call | tf_op jit(solution)/shard_map/twins/pallas_call | solution.py:591
  218.6 2.0 copy.6
  220.6 2.0 copy.7

commit v3 on v2

--- a/solution.py
+++ b/solution.py
@@ -11,7 +11,7 @@
 off_weight = 0.0051
 LANES = 128
 SUBLANES = 8
-HALVES = 1
+HALVES = 2
 PARTS = 2
 BLOCK = 256
 VMEM_LIMIT = 50 << 20
@@ -79,6 +79,9 @@
     sums_send_sem,
     sums_recv_sem,
     load_sem,
+    last_in,
+    last_send_sem,
+    last_recv_sem,
 ):
     rows, width = a_high.shape
     chunks = width // LANES
@@ -109,9 +112,10 @@
     share = size[-1]
 
     barrier = pltpu.get_barrier_semaphore()
-    for device in [near, ahead, behind] + peer:
+    others = [(group, lax.rem(row + d, row_devices)) for d in range(1, row_devices)]
+    for device in [near, ahead, behind] + others:
         pl.semaphore_signal(barrier, inc=1, device_id=device, device_id_type=MESH)
-    pl.semaphore_wait(barrier, 3 + bits)
+    pl.semaphore_wait(barrier, 3 + len(others))
 
     def remote(source, target, send, recv, device):
         return pltpu.make_async_remote_copy(
@@ -543,10 +547,23 @@
     lax.fori_loop(0, rows // LANES, finish_a, 0)
     for chunk in range(chunks - 2, chunks):
         end_b(chunk)
-    for b in range(bits):
-        sums_copy(2, b).start()
-        sums_copy(2, b).wait()
-        sums[2, b + 1] = sums[2, b] + sums_in[2, b]
+    last = [
+        remote(
+            sums.at[2, 0],
+            last_in.at[d],
+            last_send_sem.at[d],
+            last_recv_sem.at[d],
+            device,
+        )
+        for d, device in enumerate(others)
+    ]
+    for copy in last:
+        copy.start()
+    total = sums[2, 0]
+    for d, copy in enumerate(last):
+        copy.wait_recv()
+        total = total + last_in[d]
+    sums[2, bits] = total
     for chunk in range(chunks):
         at = pl.ds(chunk * LANES, LANES)
         end_mean = sums[2, bits, 0:1, at] / batch
@@ -561,6 +578,8 @@
 
         lax.fori_loop(0, PARTS, finish_b, 0)
 
+    for copy in last:
+        copy.wait_send()
     stat_near().wait_send()
     stat_ahead().wait_send()
 
@@ -629,6 +648,9 @@
             dma((3, bits)),
             dma((3, bits)),
             dma((1 + chunks,)),
+            pltpu.VMEM((row_devices - 1, SUBLANES, width), f32),
+            dma((row_devices - 1,)),
+            dma((row_devices - 1,)),
         ],
         compiler_params=pltpu.CompilerParams(
             collective_id=0, has_side_effects=True, vmem_limit_bytes=VMEM_LIMIT

time: 223 us -> 222 us (level)
  no operation moved by 1% of the time
where the time goes in v3:
time: 222 us; the launch traced here: 221 us
  Pallas kernels  217 us (98%)
  local copies, waits for them, and re-layouts  4.03 us (2%)
    pallas_call x1, Pallas kernels, per_device(): pl.pallas_call(functools.partial(kernel, groups, row_devices), out_shape=...  217 us

profile of v3, /device:TPU:0, one launch (start us, length us, event | category | flops | bytes accessed | tf_op | source)
XLA Modules:
  0.0 221.3 jit_solution(18041183237093345411)
XLA Ops:
  0.6 216.7 %twins.1 = (f32[1024,1024]{1,0:T(8,128)S(1)}, f32[1024,1024]{1,0:T(8,128)S(1)}) custom-call(f32[1024,1024]{1,0:T(8,128)} %view_a.1, f32[1024,1024]{1,0:T(8,128)} %view_b.1), custom_call_target="tpu_custom_call" | custom-call | tf_op jit(solution)/shard_map/twins/pallas_call | solution.py:610
  217.3 2.0 copy.6
  219.3 2.0 copy.7

commit v4 on v3

--- a/solution.py
+++ b/solution.py
@@ -13,7 +13,7 @@
 SUBLANES = 8
 HALVES = 2
 PARTS = 2
-BLOCK = 256
+BLOCK = 512
 VMEM_LIMIT = 50 << 20
 HOLD = 2
 WINDOW = 1

time: 222 us -> 283 us (1.27)
  Pallas kernels: 217 us -> 278 us
    pallas_call x1, Pallas kernels: 217 us -> 278 us  [per_device(): pl.pallas_call(functools.partial(kernel, groups, row_devices), out_shape=...]
where the time goes in v4:
time: 283 us
  Pallas kernels  278 us (98%)
  local copies, waits for them, and re-layouts  4.03 us (1%)
    pallas_call x1, Pallas kernels, per_device(): pl.pallas_call(functools.partial(kernel, groups, row_devices), out_shape=...  278 us

profile of v4, /device:TPU:0, one launch (start us, length us, event | category | flops | bytes accessed | tf_op | source)
XLA Modules:
  0.0 283.0 jit_solution(4011446598978829627)
XLA Ops:
  0.6 278.3 %twins.1 = (f32[1024,1024]{1,0:T(8,128)S(1)}, f32[1024,1024]{1,0:T(8,128)S(1)}) custom-call(f32[1024,1024]{1,0:T(8,128)} %view_a.1, f32[1024,1024]{1,0:T(8,128)} %view_b.1), custom_call_target="tpu_custom_call" | custom-call | tf_op jit(solution)/shard_map/twins/pallas_call | solution.py:610
  279.0 2.0 copy.6
  281.0 2.0 copy.7
